TPU v7x, 32 devices: a whole 2x2x4 slice. The times are simulated.
32 devices in a mesh: groups: 2 (over y), chan: 4 (over z), freq: 2 (over x), win: 2 (over core).
Axes of the slice: x: 2, y: 2, z: 4, core: 2. Of those that a mesh axis runs over, the one named last changes fastest.
Arguments:
- record: bfloat16 [16, 2048, 1000], P(('groups', 'chan', 'win'), 'freq'), parts along dimension 0, may hold values from -50 to 50, as said below
- pair_list: int32 [8192, 2], P(('groups', 'chan')), parts along dimension 0, may hold values from -1 to 2047, as said below
Outputs:
- correlation: float32 [8192, 1000], P(('groups', 'chan', 'freq', 'win')), parts along dimension 0
There are 2 independent parts, one for each index of `groups`. A program takes and returns all parts, laid end to end along the dimension named above; each array names one. Nothing has to cross between parts.
Inputs may be any that keep to these rules, and one draw needn't show every extreme that they name: `record`: channel gains differ strongly from channel to channel. `pair_list`: slot r belongs to block j = r // 1024. A live slot holds a channel of block j (channels j * 512 to (j + 1) * 512 - 1) and a different channel at most 256 positions from it; an empty slot holds -1 twice. Empty slots of a block come after all its live ones; every block has 512 or more live slots and some block has all 1024 live.
All inputs are finite; a program needn't handle non-finite values.
Results may differ from a plain program's by a relative error of at most 0.0052.
Values may be sent and summed in bfloat16 or wider, within the bound.
A program may use at most 64 MiB of HBM per device.

v0:
```python
import math

import jax
import jax.numpy as jnp
from jax import lax
from jax.sharding import PartitionSpec as P

SAMPLES = 1000
FFT_LEN = 1024
BINS = 512
LAGS = 1000
SMOOTH = 8
SPAN = 256


floor_level = 0.5


def extended_2(cells, sides, width):
    for axis, dim in sides:
        count = lax.axis_size(axis)
        ends = count - 1
        head = lax.slice_in_dim(cells, 0, width, axis=dim)
        tail = lax.slice_in_dim(cells, cells.shape[dim] - width, cells.shape[dim], axis=dim)
        cells = jnp.concatenate(
            [
                lax.ppermute(tail, axis, [(i, (i + 1) % count) for i in range(ends)]),
                cells,
                lax.ppermute(head, axis, [((i + 1) % count, i) for i in range(ends)]),
            ],
            axis=dim,
        )
    return cells


def dft_parts(bin_index):
    samples = jnp.arange(SAMPLES, dtype=jnp.int32)
    angles = jnp.mod(samples[:, None] * bin_index[None, :], FFT_LEN).astype(jnp.float32) * (
        2.0 * math.pi / FFT_LEN
    )
    factor = 1.0 / math.sqrt(FFT_LEN)
    return (jnp.cos(angles) * factor, -jnp.sin(angles) * factor)


def lag_columns(bin_index, factor):
    lag_index = jnp.arange(LAGS, dtype=jnp.int32) - LAGS // 2
    angles = jnp.mod(bin_index[:, None] * lag_index[None, :], FFT_LEN).astype(jnp.float32) * (
        2.0 * math.pi / FFT_LEN
    )
    return jnp.concatenate([jnp.cos(angles) * factor, -jnp.sin(angles) * factor], axis=0)


def smooth_amplitude(amplitude):
    width = amplitude.shape[-1]
    padded = jnp.pad(amplitude, [(0, 0)] * (amplitude.ndim - 1) + [(SMOOTH, SMOOTH)])
    summed = padded[..., 0:width]
    for step in range(1, 2 * SMOOTH + 1):
        summed = summed + padded[..., step : step + width]
    bins = jnp.arange(1, width + 1, dtype=jnp.int32)
    counts = (jnp.minimum(bins + SMOOTH, width) - jnp.maximum(bins - SMOOTH, 1) + 1).astype(
        jnp.float32
    )
    return summed / counts


def whiten(spec_re, spec_im):
    amplitude = jnp.sqrt(spec_re * spec_re + spec_im * spec_im)
    divisor = jnp.maximum(smooth_amplitude(amplitude), floor_level)
    return (spec_re / divisor, spec_im / divisor)


def body(record, pair_list):
    win_local, chan_local, sample_len = record.shape
    freq_size = lax.axis_size("freq")
    chan_size = lax.axis_size("chan")
    win_size = lax.axis_size("win")
    bin_count = BINS // freq_size
    row_total = win_local * chan_local
    bin_index = 1 + jnp.arange(BINS, dtype=jnp.int32)
    cos_part, sin_part = dft_parts(bin_index)
    dft_table = jnp.stack(
        [
            cos_part.reshape(sample_len, freq_size, bin_count),
            sin_part.reshape(sample_len, freq_size, bin_count),
        ],
        axis=2,
    )
    dft_table = dft_table.reshape(sample_len, 2 * BINS).astype(jnp.bfloat16)
    spectrum = jnp.dot(
        record.reshape(row_total, sample_len), dft_table, preferred_element_type=jnp.float32
    )
    spectrum = spectrum.reshape(row_total, freq_size, 2, bin_count)
    white_re, white_im = whiten(
        spectrum[:, :, 0].reshape(row_total, BINS), spectrum[:, :, 1].reshape(row_total, BINS)
    )
    whitened = jnp.stack(
        [
            white_re.reshape(row_total, freq_size, bin_count),
            white_im.reshape(row_total, freq_size, bin_count),
        ],
        axis=2,
    )
    whitened = whitened.astype(jnp.bfloat16).reshape(
        win_local, chan_local, freq_size, 2 * bin_count
    )
    block_len = chan_local * freq_size // chan_size
    own_block = lax.all_to_all(
        lax.all_to_all(whitened, "freq", split_axis=2, concat_axis=1, tiled=True),
        "chan",
        split_axis=1,
        concat_axis=0,
        tiled=True,
    )
    own_block = own_block.reshape(win_local * chan_size, block_len, 2 * bin_count)
    extended = extended_2(own_block, (("chan", 1),), SPAN)
    offset_base = lax.axis_index("chan") * block_len - SPAN
    live_slot = pair_list[:, 0] >= 0
    left_index = jnp.where(live_slot, pair_list[:, 0] - offset_base, 0)
    right_index = jnp.where(live_slot, pair_list[:, 1] - offset_base, 0)
    left_rows = jnp.take(extended, left_index, axis=1)
    right_rows = jnp.take(extended, right_index, axis=1)
    left_re, left_im = (left_rows[..., :bin_count], left_rows[..., bin_count:])
    right_re, right_im = (right_rows[..., :bin_count], right_rows[..., bin_count:])
    cross_re = jnp.einsum(
        "wpk,wpk->pk", left_re, right_re, preferred_element_type=jnp.float32
    ) + jnp.einsum("wpk,wpk->pk", left_im, right_im, preferred_element_type=jnp.float32)
    cross_im = jnp.einsum(
        "wpk,wpk->pk", left_im, right_re, preferred_element_type=jnp.float32
    ) - jnp.einsum("wpk,wpk->pk", left_re, right_im, preferred_element_type=jnp.float32)
    cross = jnp.concatenate([cross_re, cross_im], axis=1) * live_slot.astype(jnp.float32)[:, None]
    windows = win_local * chan_size * win_size
    my_bins = lax.axis_index("freq") * bin_count + 1 + jnp.arange(bin_count, dtype=jnp.int32)
    lag_table = lag_columns(my_bins, 1.0 / math.sqrt(windows * BINS))
    return lax.psum_scatter(
        jnp.dot(
            cross, lag_table, precision=lax.Precision.HIGHEST, preferred_element_type=jnp.float32
        ),
        ("freq", "win"),
        scatter_dimension=0,
        tiled=True,
    )


def solution(mesh):
    in_specs = (P(("groups", "chan", "win"), "freq", None), P(("groups", "chan"), None))
    out_specs = P(("groups", "chan", "freq", "win"), None)
    return jax.shard_map(body, mesh=mesh, in_specs=in_specs, out_specs=out_specs, check_vma=False)
```

profile of v0, /device:TPU:9, one launch (start us, length us, event | category | flops | bytes accessed | tf_op | source)
XLA Modules:
  0.0 288.2 jit_solution(13364023434503692544)
XLA Ops:
  6.6 8.5 %multiply_convert_fusion.1 = (bf16[1000,2,1,256]{3,0,2,1:T(8,128)(2,1)S(1)}, bf16[1000,2,1,256]{3,0,2,1:T(8,128)(2,1)S(1)}) fusion(s32[2,256]{1,0:T(2,128)S(1)} %add_add_fusion), kind=kLoop, calls=%fused_computation.56 | loop fusion | flops 9728000 | bytes 2050048 | tf_op jit(solution)/shard_map/convert.5
  16.5 3.9 %copy.19 = bf16[1000,2,2,256]{0,3,2,1:T(8,128)(2,1)} copy(bf16[1000,2,2,256]{3,0,2,1:T(8,128)(2,1)} %pad_maximum_fusion.1) | data formatting | bytes 4096000 | tf_op jit(solution)/shard_map/stack | solution.py:81
  20.4 3.9 %fusion.23 = f32[1024,1024]{1,0:T(8,128)S(1)} fusion(bf16[1000,1024]{0,1:T(8,128)(2,1)} %bitcast.83, bf16[1,1024,1000]{1,2,0:T(8,128)(2,1)S(1)} %copy-done), kind=kOutput, calls=%fused_computation.53 | convolution fusion | flops 2097152000 | bytes 8290304 | tf_op jit(solution)/shard_map/dot_general | solution.py:89
  25.7 3.7 %fusion.13 = (bf16[1024,512]{0,1:T(8,128)(2,1)S(1)}, f32[1024,512]{0,1:T(8,128)S(1)}) fusion(f32[1024,2,1,256]{0,3,2,1:T(8,128)S(1)} %get-tuple-element.13, f32[512]{0:T(512)S(1)} %add_convert_fusion, f32[1024,512]{0,1:T(8,128)S(1)} %fusion.11), kind=kLoop, calls=%fused_computation.34 | loop fusion | flops 10485760 | bytes 7342080 | tf_op jit(solution)/shard_map/convert.4
  30.1 27.6 %all_to_all.27 = bf16[1,1024,2,512]{1,3,0,2:T(8,128)(2,1)} all-to-all(bf16[1,1024,2,512]{1,3,0,2:T(8,128)(2,1)S(1)} %bitcast.79), channel_id=1, replica_groups=mesh['groups'=2,'chan'=4,'freq'=2,'win'=2] {'freq'}, dimensions={2} | all-to-all | bytes 4194304 | tf_op jit(solution)/shard_map/all_to_all | solution.py:108
  57.7 4.0 %copy.21 = bf16[1,1024,2,512]{3,1,2,0:T(8,128)(2,1)} copy(bf16[1,1024,2,512]{1,3,0,2:T(8,128)(2,1)} %all_to_all.27) | data formatting | bytes 4194304 | tf_op jit(solution)/shard_map/all_to_all | solution.py:108
  61.7 7.5 %copy.59 = bf16[1,2048,1,512]{3,2,0,1:T(2,128)(2,1)} copy(bf16[1,2048,1,512]{3,1,2,0:T(8,128)(2,1)} %bitcast.78) | data formatting | bytes 4194304 | tf_op jit(solution)/shard_map/all_to_all | solution.py:108
  69.7 15.4 %reduce.8 = bf16[2048,512]{1,0:T(8,128)(2,1)} reduce(bf16[2048,1,1,512]{3,2,1,0:T(2,128)(2,1)} %bitcast.76, bf16[]{:T(256)} %broadcast.224), dimensions={1,2}, to_apply=%bitcast.73.reduce_sub_computation | reduce | bytes 4194306
  85.0 4.5 %reshape.190 = bf16[4,2,131072]{2,1,0:T(2,128)(2,1)} reshape(bf16[2048,512]{1,0:T(8,128)(2,1)} %reduce.8) | data formatting | bytes 4194304
  89.5 4.9 %all-to-all-start.1 = ((bf16[4,2,131072]{2,1,0:T(2,128)(2,1)}), bf16[4,2,131072]{2,1,0:T(2,128)(2,1)}, u32[]{:S(2)}, u32[]{:S(2)}) async-start(bf16[4,2,131072]{2,1,0:T(2,128)(2,1)} %reshape.190), calls=%async_computation.1 | async-start | bytes 4194304 | tf_op jit(solution)/shard_map/all_to_all | solution.py:107
  94.5 43.4 %all-to-all-done.1 = bf16[4,2,131072]{2,1,0:T(2,128)(2,1)} async-done(((bf16[4,2,131072]{2,1,0:T(2,128)(2,1)}), bf16[4,2,131072]{2,1,0:T(2,128)(2,1)}, u32[]{:S(2)}, u32[]{:S(2)}) %all-to-all-start.1) | async-done | bytes 2097184 | tf_op jit(solution)/shard_map/all_to_all | solution.py:107
  137.9 4.9 %reshape.191 = bf16[2048,1,1,512]{3,2,1,0:T(2,128)(2,1)} reshape(bf16[4,2,131072]{2,1,0:T(2,128)(2,1)} %all-to-all-done.1) | data formatting | bytes 4194304
  146.7 4.4 %collective-permute-start = (bf16[4,256,512]{2,0,1:T(4,128)(2,1)S(1)}, bf16[4,256,512]{2,0,1:T(4,128)(2,1)S(1)}, u32[]{:S(2)}, u32[]{:S(2)}) collective-permute-start(bf16[4,256,512]{2,0,1:T(4,128)(2,1)S(1)} %copy.56), channel_id=1, source_target_pairs={{0,4},{4,8},{8,12},{1,5},{5,9},{9,13},{2,6},{6,10},{10,14},{3,7},{... | collective-permute-start | bytes 3145736 | tf_op jit(solution)/shard_map/ppermute | solution.py:27
  151.9 3.3 %collective-permute-start.1 = (bf16[4,256,512]{2,0,1:T(4,128)(2,1)S(1)}, bf16[4,256,512]{2,0,1:T(4,128)(2,1)S(1)}, u32[]{:S(2)}, u32[]{:S(2)}) collective-permute-start(bf16[4,256,512]{2,0,1:T(4,128)(2,1)S(1)} %copy.57), channel_id=1, source_target_pairs={{4,0},{8,4},{12,8},{5,1},{9,5},{13,9},{6,2},{10,6},{14,10},{7,3},{... | collective-permute-start | bytes 3145736 | tf_op jit(solution)/shard_map/ppermute | solution.py:29
  155.2 5.2 %cosine_multiply_fusion = (f32[256,1000]{1,0:T(8,128)S(1)}, f32[256,1000]{1,0:T(8,128)}) fusion(s32[1000]{0:T(1024)S(1)} %iota_add_fusion, s32[256]{0:T(256)S(1)} %iota_add_fusion.1), kind=kLoop, calls=%fused_computation.69 | loop fusion | flops 4352000 | bytes 2053024 | tf_op jit(solution)/shard_map/mul | solution.py:50
  160.4 14.0 %collective-permute-done = bf16[4,256,512]{2,0,1:T(4,128)(2,1)S(1)} collective-permute-done((bf16[4,256,512]{2,0,1:T(4,128)(2,1)S(1)}, bf16[4,256,512]{2,0,1:T(4,128)(2,1)S(1)}, u32[]{:S(2)}, u32[]{:S(2)}) %collective-permute-start) | collective-permute-done | bytes 1048608 | tf_op jit(solution)/shard_map/ppermute | solution.py:27
  175.9 2.9 %constant_dynamic-update-slice_fusion.1 = bf16[4,1024,512]{2,0,1:T(4,128)(2,1)} fusion(bf16[4,1024,512]{2,0,1:T(4,128)(2,1)} %constant_dynamic-update-slice_fusion.2, bf16[4,512,512]{2,1,0:T(8,128)(2,1)S(1)} %bitcast.75), kind=kLoop, calls=%fused_computation.74 | loop fusion | bytes 4194304
  180.2 13.0 %gather_fusion.1 = bf16[1024,4,512]{2,1,0:T(4,128)(2,1)} fusion(bf16[4,1024,512]{2,0,1:T(4,128)(2,1)} %constant_dynamic-update-slice_fusion, s32[1024]{0:T(1024)S(1)} %get-tuple-element.23), kind=kCustom, calls=%fused_computation.1.clone | custom fusion | bytes 8392704 | tf_op jit(solution)/shard_map/jit(_take)/gather | solution.py:121
  193.2 12.9 %gather_fusion = bf16[1024,4,512]{2,1,0:T(4,128)(2,1)} fusion(bf16[4,1024,512]{2,0,1:T(4,128)(2,1)} %constant_dynamic-update-slice_fusion, s32[1024]{0:T(1024)S(1)} %get-tuple-element.22), kind=kCustom, calls=%fused_computation.clone | custom fusion | bytes 8392704 | tf_op jit(solution)/shard_map/jit(_take)/gather | solution.py:120
  206.1 5.4 %select_bitcast_fusion = bf16[4,1024,512]{2,0,1:T(4,128)(2,1)S(1)} fusion(bf16[1024,4,512]{2,1,0:T(4,128)(2,1)} %gather_fusion.1, pred[1024]{0:T(1024)(128)(4,1)S(1)} %compare_and_fusion), kind=kLoop, calls=%fused_computation.10 | loop fusion | flops 2097152 | bytes 8389632 | tf_op jit(solution)/shard_map/jit(_take)/select_n | solution.py:121
  211.6 3.9 %select_bitcast_fusion.1 = bf16[4,1024,512]{2,0,1:T(4,128)(2,1)S(1)} fusion(bf16[1024,4,512]{2,1,0:T(4,128)(2,1)S(1)} %copy-done.2, pred[1024]{0:T(1024)(128)(4,1)S(1)} %compare_and_fusion.1), kind=kLoop, calls=%fused_computation.11 | loop fusion | flops 2097152 | bytes 8389632 | tf_op jit(solution)/shard_map/jit(_take)/select_n | solution.py:120
  215.5 11.3 %fusion.2 = (f32[1024,256]{1,0:T(8,128)S(1)}, f32[1024,256]{1,0:T(8,128)S(1)}, f32[1024,256]{1,0:T(8,128)S(1)}, f32[1024,256]{1,0:T(8,128)S(1)}) fusion(bf16[4,1024,512]{2,0,1:T(4,128)(2,1)S(1)} %select_bitcast_fusion.1, bf16[4,1024,512]{2,0,1:T(4,128)(2,1)S(1)} %select_bitcast_fusion), kind=kLoop, calls=%fused_computation.8 | loop fusion | flops 11534336 | bytes 12582912 | tf_op jit(solution)/shard_map/wpk,wpk->pk/dot_general | solution.py:126
  228.2 9.0 %fusion.4 = f32[1024,1000]{0,1:T(8,128)} fusion(f32[1024,256]{1,0:T(8,128)S(1)} %sub.41, f32[1024,256]{1,0:T(8,128)S(1)} %add.167, f32[256,1000]{1,0:T(8,128)S(1)} %copy-done.3, f32[256,1000]{1,0:T(8,128)S(1)} %get-tuple-element.18, f32[1024]{0:T(1024)S(1)} %bitcast.84), kind=kOutput, calls=%fused_computation.21 | convolution fusion | flops 6293016576 | bytes 8245248 | tf_op jit(solution)/shard_map/dot_general | solution.py:135
  237.3 44.1 %reduce-scatter.2.cloned.1.call-done = f32[256,1000]{0,1:T(8,128)} async-done(((f32[1024,1000]{0,1:T(8,128)}), f32[256,1000]{0,1:T(8,128)}) %reduce-scatter.2.cloned.1.call-update) | async-done | bytes 1024016 | tf_op jit(solution)/shard_map/reduce_scatter | solution.py:134
  (36 shorter events, 12.7 us)
Async XLA Ops:
  6.5 13.9 %copy-start = (bf16[1,1024,1000]{1,2,0:T(8,128)(2,1)S(1)}, bf16[1,1024,1000]{1,2,0:T(8,128)(2,1)}, u32[]{:S(2)}) copy-start(bf16[1,1024,1000]{1,2,0:T(8,128)(2,1)} %param.4) | copy-start | bytes 6144004
  89.5 4.9 %copy-start.4 = (s32[1024,2]{0,1:T(2,128)S(1)}, s32[1024,2]{0,1:T(2,128)}, u32[]{:S(2)}) copy-start(s32[1024,2]{0,1:T(2,128)} %param.5) | copy-start | bytes 24580
  89.5 48.4 %all-to-all-start.1 = ((bf16[4,2,131072]{2,1,0:T(2,128)(2,1)}), bf16[4,2,131072]{2,1,0:T(2,128)(2,1)}, u32[]{:S(2)}, u32[]{:S(2)}) async-start(bf16[4,2,131072]{2,1,0:T(2,128)(2,1)} %reshape.190), calls=%async_computation.1 | async-start | bytes 4194304 | tf_op jit(solution)/shard_map/all_to_all | solution.py:107
  94.4 186.9 %reduce-scatter.2.cloned.1.call-start = ((), (), s32[]{:S(2)}) async-start(), calls=%async_computation.3 | async-start | bytes 5120000 | tf_op jit(solution)/shard_map/reduce_scatter | solution.py:134
  146.7 27.8 %collective-permute-start = (bf16[4,256,512]{2,0,1:T(4,128)(2,1)S(1)}, bf16[4,256,512]{2,0,1:T(4,128)(2,1)S(1)}, u32[]{:S(2)}, u32[]{:S(2)}) collective-permute-start(bf16[4,256,512]{2,0,1:T(4,128)(2,1)S(1)} %copy.56), channel_id=1, source_target_pairs={{0,4},{4,8},{8,12},{1,5},{5,9},{9,13},{2,6},{6,10},{10,14},{3,7},{... | collective-permute-start | bytes 3145736 | tf_op jit(solution)/shard_map/ppermute | solution.py:27
  151.9 26.9 %collective-permute-start.1 = (bf16[4,256,512]{2,0,1:T(4,128)(2,1)S(1)}, bf16[4,256,512]{2,0,1:T(4,128)(2,1)S(1)}, u32[]{:S(2)}, u32[]{:S(2)}) collective-permute-start(bf16[4,256,512]{2,0,1:T(4,128)(2,1)S(1)} %copy.57), channel_id=1, source_target_pairs={{4,0},{8,4},{12,8},{5,1},{9,5},{13,9},{6,2},{10,6},{14,10},{7,3},{... | collective-permute-start | bytes 3145736 | tf_op jit(solution)/shard_map/ppermute | solution.py:29
  206.1 5.5 %copy-start.2 = (bf16[1024,4,512]{2,1,0:T(4,128)(2,1)S(1)}, bf16[1024,4,512]{2,1,0:T(4,128)(2,1)}, u32[]{:S(2)}) copy-start(bf16[1024,4,512]{2,1,0:T(4,128)(2,1)} %gather_fusion) | copy-start | bytes 12582916
  227.0 1.2 copy-start.3
  228.2 53.1 %copy-start.1 = (bf16[1,1024,1000]{1,2,0:T(8,128)(2,1)S(1)}, bf16[1,1024,1000]{1,2,0:T(8,128)(2,1)}, u32[]{:S(2)}) copy-start(bf16[1,1024,1000]{1,2,0:T(8,128)(2,1)} %param.4) | copy-start | bytes 6144004
Sparse Core Ops, SparseCore 0:
  237.4 43.8 reduce-scatter.1
where the time goes:
time: 291 us; the launch traced here: 288 us
  waiting for transfers between devices  102 us (35%)
  local copies, waits for them, and re-layouts  63.2 us (22%)
  other arithmetic  56.7 us (19%)
  blocking collectives  27.6 us (9%)
  between operations  13.6 us (5%)
  matrix products  12.9 us (4%)
  starting transfers between devices  12.5 us (4%)
    reduce_scatter x1, waiting for transfers between devices, body(): lax.psum_scatter(jnp.dot(cross, lag_table, precision=lax.Precision.HIGHES...  44.1 us
    all_to_all x1, waiting for transfers between devices, body(): lax.all_to_all(lax.all_to_all(whitened, 'freq', split_axis=2, concat_axis...  43.4 us
    all_to_all x1, blocking collectives, body(): lax.all_to_all(whitened, 'freq', split_axis=2, concat_axis=1, tiled=True)  27.6 us
    unnamed x18, local copies, waits for them, and re-layouts  19.8 us
    unnamed x1, other arithmetic  15.4 us
    ppermute x1, waiting for transfers between devices, extended_2(): lax.ppermute(tail, axis, [(i, (i + 1) % count) for i in range(ends)])  14 us
    gather x1, local copies, waits for them, and re-layouts, body(): right_rows = jnp.take(extended, right_index, axis=1)  13 us
    gather x1, local copies, waits for them, and re-layouts, body(): left_rows = jnp.take(extended, left_index, axis=1)  12.9 us
  transfers between devices with their start and end apart: 4, of which 3 were waited for; matrix products, arithmetic and copies ran while one was open for 4% of the time, Pallas kernels for 0%

commit v1 on v0

v1 whole, which is shorter than its diff:
```python
import functools
import math

import jax
import jax.numpy as jnp
import numpy as np
from jax import lax
from jax.experimental import pallas as pl
from jax.experimental.pallas import tpu as pltpu
from jax.sharding import PartitionSpec as P

SAMPLES = 1000
FFT_LEN = 1024
BINS = 512
LAGS = 1000
SMOOTH = 8
SPAN = 256
FLOOR = 0.5


def dft_table():
    bins = 1 + np.arange(BINS)
    angles = ((np.arange(SAMPLES)[:, None] * bins[None, :]) % FFT_LEN) * (2.0 * np.pi / FFT_LEN)
    table = np.concatenate([np.cos(angles), -np.sin(angles)], axis=1) / math.sqrt(FFT_LEN)
    return jnp.asarray(table.astype(np.float32)).astype(jnp.bfloat16)


def smoothing():
    bins = np.arange(BINS)
    band = (np.abs(bins[:, None] - bins[None, :]) <= SMOOTH).astype(np.float32)
    return band, (1.0 / band.sum(axis=0, keepdims=True)).astype(np.float32)


def rotation(windows):
    bins = 1 + np.arange(BINS)
    angles = ((bins * (LAGS // 2)) % FFT_LEN) * (2.0 * np.pi / FFT_LEN)
    scale = math.sqrt(FFT_LEN) / math.sqrt(windows * BINS)
    return (np.stack([np.cos(angles), np.sin(angles)]) * scale).astype(np.float32)


def whiten_rows(rows, table, band, inverse):
    spectrum = jnp.dot(rows, table, preferred_element_type=jnp.float32)
    spec_re, spec_im = spectrum[:, :BINS], spectrum[:, BINS:]
    amplitude = jnp.sqrt(spec_re * spec_re + spec_im * spec_im)
    high = amplitude.astype(jnp.bfloat16)
    low = (amplitude - high.astype(jnp.float32)).astype(jnp.bfloat16)
    summed = jnp.dot(high, band, preferred_element_type=jnp.float32) + jnp.dot(
        low, band, preferred_element_type=jnp.float32
    )
    factor = 1.0 / jnp.maximum(summed * inverse, FLOOR)
    return (spec_re * factor).astype(jnp.bfloat16), (spec_im * factor).astype(jnp.bfloat16)


def whiten_kernel(parts, x_ref, table_ref, band_ref, inverse_ref, out_ref):
    count = BINS // parts
    white_re, white_im = whiten_rows(x_ref[...], table_ref[...], band_ref[...], inverse_ref[...])
    for q in range(parts):
        out_ref[q, :, 0:count] = white_re[:, q * count : (q + 1) * count]
        out_ref[q, :, count : 2 * count] = white_im[:, q * count : (q + 1) * count]


def cross_rows(left_index, right_index, block, left_data, right_data, base, rot, wins):
    length = left_data.shape[0]
    reach = right_data.shape[0]
    count = rot.shape[1]
    start = block * length
    own = jnp.logical_and(left_index >= start, left_index < start + length)
    first = jnp.where(own, left_index, right_index) - start
    second = jnp.where(own, right_index, left_index) - base
    sign = jnp.where(own, 1.0, -1.0)
    slots = left_index.shape[0]
    one_left = jnp.where(
        lax.broadcasted_iota(jnp.int32, (slots, length), 1) == first, 1.0, 0.0
    ).astype(jnp.bfloat16)
    one_right = jnp.where(
        lax.broadcasted_iota(jnp.int32, (slots, reach), 1) == second, 1.0, 0.0
    ).astype(jnp.bfloat16)
    left = jnp.dot(one_left, left_data, preferred_element_type=jnp.float32)
    right = jnp.dot(one_right, right_data, preferred_element_type=jnp.float32)
    real = imag = 0.0
    for w in range(wins):
        at = 2 * count * w
        left_re, left_im = left[:, at : at + count], left[:, at + count : at + 2 * count]
        right_re, right_im = right[:, at : at + count], right[:, at + count : at + 2 * count]
        real = real + (left_re * right_re + left_im * right_im)
        imag = imag + (left_im * right_re - left_re * right_im)
    imag = imag * sign
    cosine, sine = rot[0:1], rot[1:2]
    return real * cosine + imag * sine, imag * cosine - real * sine


def cross_kernel(wins, length, reach, tile, pair_ref, data_ref, rot_ref, out_ref):
    block = pl.program_id(0)
    channels = data_ref.shape[0]
    base = pl.multiple_of(
        jnp.clip(block * length - SPAN, 0, channels - reach), math.gcd(SPAN, length)
    )
    start = pl.multiple_of(block * length, length)
    left_data = data_ref[pl.ds(start, length), :]
    right_data = data_ref[pl.ds(base, reach), :]
    count = rot_ref.shape[1]
    for at in range(0, pair_ref.shape[0], tile):
        real, imag = cross_rows(
            pair_ref[at : at + tile, 0:1],
            pair_ref[at : at + tile, 1:2],
            block,
            left_data,
            right_data,
            base,
            rot_ref[...],
            wins,
        )
        out_ref[0, at : at + tile, 0:count] = real.astype(jnp.bfloat16)
        out_ref[0, at : at + tile, count : 2 * count] = imag.astype(jnp.bfloat16)


def exchange(pieces, axes, size):
    me = lax.axis_index(axes)
    out = []
    for step in range(size):
        perm = [(i, i ^ step) for i in range(size)]
        piece = lax.dynamic_index_in_dim(pieces, me ^ step, 0, keepdims=False)
        out.append(piece if step == 0 else lax.ppermute(piece, axes, perm))
    return out


def body(record, pair_list):
    win_local, chan_local, samples = record.shape
    chan_size, freq_size, win_size = (lax.axis_size(a) for a in ("chan", "freq", "win"))
    parts = freq_size * win_size
    axes = ("freq", "win")
    count = BINS // parts
    windows = win_local * chan_size * win_size
    channels = chan_local * freq_size
    length = channels // chan_size
    reach = length + 2 * SPAN
    slots = pair_list.shape[0]
    me = lax.axis_index(axes)
    table = dft_table()
    band, inverse = smoothing()
    tile = 256
    whitened = pl.pallas_call(
        functools.partial(whiten_kernel, parts),
        grid=(chan_local // tile,),
        in_specs=[
            pl.BlockSpec((tile, samples), lambda i: (i, 0)),
            pl.BlockSpec((samples, 2 * BINS), lambda i: (0, 0)),
            pl.BlockSpec((BINS, BINS), lambda i: (0, 0)),
            pl.BlockSpec((1, BINS), lambda i: (0, 0)),
        ],
        out_specs=pl.BlockSpec((parts, tile, 2 * count), lambda i: (0, i, 0)),
        out_shape=jax.ShapeDtypeStruct((parts, chan_local, 2 * count), jnp.bfloat16),
    )(record.reshape(chan_local, samples), table, jnp.asarray(band, jnp.bfloat16), inverse)
    pairs = lax.all_gather(pair_list, "chan", axis=0, tiled=True)
    if parts & (parts - 1) == 0:
        got = exchange(whitened, axes, parts)
    stacked = jnp.stack(got)
    order = jnp.arange(parts) ^ me
    data = jnp.take(stacked, order, axis=0)
    data = data.reshape(freq_size, win_size, chan_local, 2 * count)
    data = data.transpose(0, 2, 1, 3).reshape(channels, win_size * 2 * count)
    rot = jnp.asarray(rotation(windows)).reshape(2, parts, count)
    rot = lax.dynamic_index_in_dim(rot, me, 1, keepdims=False)
    cross = pl.pallas_call(
        functools.partial(cross_kernel, win_size, length, reach, tile),
        grid=(chan_size,),
        in_specs=[
            pl.BlockSpec((slots, 2), lambda i: (i, 0)),
            pl.BlockSpec((channels, win_size * 2 * count), lambda i: (0, 0)),
            pl.BlockSpec((2, count), lambda i: (0, 0)),
        ],
        out_specs=pl.BlockSpec((1, slots, 2 * count), lambda i: (i, 0, 0)),
        out_shape=jax.ShapeDtypeStruct((chan_size, slots, 2 * count), jnp.bfloat16),
    )(pairs, data, rot)
    c = lax.axis_index("chan")

    def block_of(d):
        return lax.dynamic_index_in_dim(cross, jnp.clip(d, 0, chan_size - 1), 0, keepdims=False)

    right = left = None
    for t in range(1, chan_size):
        send_right = block_of(chan_size - t + c)
        send_left = block_of(t - chan_size + c)
        if right is not None:
            send_right = (send_right.astype(jnp.float32) + right.astype(jnp.float32)).astype(
                jnp.bfloat16
            )
            send_left = (send_left.astype(jnp.float32) + left.astype(jnp.float32)).astype(
                jnp.bfloat16
            )
        right = lax.ppermute(send_right, "chan", [(i, i + 1) for i in range(t)])
        left = lax.ppermute(
            send_left, "chan", [(i, i - 1) for i in range(chan_size - 1, chan_size - 1 - t, -1)]
        )
    total = block_of(c).astype(jnp.float32)
    total = (total + right.astype(jnp.float32) + left.astype(jnp.float32)).astype(jnp.bfloat16)
    final = exchange(total.reshape(parts, slots // parts, 2 * count), axes, parts)
    final = jnp.take(jnp.stack(final), order, axis=0)
    final = final.reshape(parts, slots // parts, 2, count).transpose(1, 2, 0, 3)
    final = final.reshape(slots // parts, 2 * BINS)
    return lax.dot_general(
        final, table, (((1,), (1,)), ((), ())), preferred_element_type=jnp.float32
    )


def solution(mesh):
    in_specs = (P(("groups", "chan", "win"), "freq", None), P(("groups", "chan"), None))
    out_specs = P(("groups", "chan", "freq", "win"), None)
    return jax.shard_map(body, mesh=mesh, in_specs=in_specs, out_specs=out_specs, check_vma=False)
```

time: 291 us -> 154 us (0.53)
  waiting for transfers between devices: 102 us -> 48.1 us
  other arithmetic: 56.7 us -> 9.36 us
  local copies, waits for them, and re-layouts: 63.2 us -> 16.2 us
  Pallas kernels: 0 us -> 18.5 us
  between operations: 13.6 us -> 0.19 us
  matrix products: 12.9 us -> 1.65 us
  blocking collectives: 27.6 us -> 38.1 us
  starting transfers between devices: 12.5 us -> 20.1 us
    reduce_scatter x1 -> x0, waiting for transfers between devices: 44.1 us -> none  [body(): lax.psum_scatter(jnp.dot(cross, lag_table, precision=lax.Precision.HIGHES...]
    all_to_all x1 -> x0, waiting for transfers between devices: 43.4 us -> none  [body(): lax.all_to_all(lax.all_to_all(whitened, 'freq', split_axis=2, concat_axis...]
    all_gather x0 -> x1, blocking collectives: none -> 38.1 us  [body(): pairs = lax.all_gather(pair_list, 'chan', axis=0, tiled=True)]
    ppermute x2 -> x12, waiting for transfers between devices: 14 us -> 48.1 us  [the longest x3 23.7 us: body(): right = lax.ppermute(send_right, 'chan', [(i, i + 1) for i in range(t)])]
    all_to_all x1 -> x0, blocking collectives: 27.6 us -> none  [body(): lax.all_to_all(whitened, 'freq', split_axis=2, concat_axis=1, tiled=True)]
    gather x2 -> x3, local copies, waits for them, and re-layouts: 25.9 us -> 2.78 us  [the longest x1 2 us: body(): data = jnp.take(stacked, order, axis=0)]
    pallas_call x0 -> x2, Pallas kernels: none -> 18.5 us  [the longest x1 11.1 us: body(): pl.pallas_call(functools.partial(cross_kernel, win_size, length, reach, t...]
    unnamed x1 -> x0, other arithmetic: 15.4 us -> none
  transfers between devices with their start and end apart: 4 -> 12, of which waited for: 3 -> 6; matrix products, arithmetic and copies ran while one was open for 4% -> 2% of each run, Pallas kernels for 0% -> 0%
where the time goes in v1:
time: 154 us; the launch traced here: 152 us
  waiting for transfers between devices  48.1 us (31%)
  blocking collectives  38.1 us (25%)
  starting transfers between devices  20.1 us (13%)
  Pallas kernels  18.5 us (12%)
  local copies, waits for them, and re-layouts  16.2 us (11%)
  other arithmetic  9.36 us (6%)
  matrix products  1.65 us (1%)
    all_gather x1, blocking collectives, body(): pairs = lax.all_gather(pair_list, 'chan', axis=0, tiled=True)  38.1 us
    ppermute x3, waiting for transfers between devices, body(): right = lax.ppermute(send_right, 'chan', [(i, i + 1) for i in range(t)])  23.7 us
    ppermute x3, waiting for transfers between devices, body(): lax.ppermute(send_left, 'chan', [(i, i - 1) for i in range(chan_size - 1,...  18.1 us
    pallas_call x1, Pallas kernels, body(): pl.pallas_call(functools.partial(cross_kernel, win_size, length, reach, t...  11.1 us
    ppermute x6, starting transfers between devices, exchange(): out.append(piece if step == 0 else lax.ppermute(piece, axes, perm))  8.27 us
    pallas_call x1, Pallas kernels, body(): pl.pallas_call(functools.partial(whiten_kernel, parts), grid=(chan_local...  7.46 us
    unnamed x11, local copies, waits for them, and re-layouts  7.45 us
    ppermute x3, starting transfers between devices, body(): right = lax.ppermute(send_right, 'chan', [(i, i + 1) for i in range(t)])  7.19 us
  transfers between devices with their start and end apart: 12, of which 6 were waited for; matrix products, arithmetic and copies ran while one was open for 2% of the time, Pallas kernels for 0%

profile of v1, /device:TPU:9, one launch (start us, length us, event | category | flops | bytes accessed | tf_op | source)
XLA Modules:
  0.0 152.3 jit_solution(8734584708616290237)
XLA Ops:
  0.0 4.0 %copy.18 = bf16[1,1024,1000]{2,1,0:T(8,128)(2,1)} copy(bf16[1,1024,1000]{1,2,0:T(8,128)(2,1)} %param.6) | data formatting | bytes 4096000 | tf_op args[0]
  4.0 7.5 %shard_map.64 = bf16[4,1024,256]{2,1,0:T(8,128)(2,1)} custom-call(bf16[1024,1000]{1,0:T(8,128)(2,1)} %bitcast.54, bf16[1000,1024]{1,0:T(8,128)(2,1)} %constant.110.table_ref, bf16[512,512]{1,0:T(8,128)(2,1)} %constant.106.clone.band_ref, f32[1,512]{1,0:T(1,128)} %constant.107.clone.inverse_ref), custom_call_target="tpu_custom_call" | custom-call | tf_op jit(solution)/shard_map/pallas_call | solution.py:142
  11.4 2.5 %constant_dynamic-slice_fusion.2 = (bf16[1,1024,256]{2,1,0:T(8,128)(2,1)S(1)}, bf16[1024,256]{1,0:T(8,128)(2,1)S(1)}, bf16[1024,256]{1,0:T(8,128)(2,1)S(1)}, bf16[1024,256]{1,0:T(8,128)(2,1)}) fusion(bf16[4,1024,256]{2,1,0:T(8,128)(2,1)} %shard_map.64, s32[]{:T(128)S(6)} %select_n.60, s32[]{:T(128)S(6)} %select_n.63, s32[]{:T(128)S(6)} %select_n.62, ...), kind=kLoop, calls=%fused_computation.28 | loop fusion | bytes 4194320 | tf_op jit(solution)/shard_map/jit(dynamic_index_in_dim)/dynamic_slice | solution.py:122
  16.4 38.1 %all_gather.3.pair_ref = s32[4096,2]{1,0:T(8,128)} all-gather(s32[1024,2]{1,0:T(8,128)S(1)} %copy.17), channel_id=1, replica_groups=mesh['groups'=2,'chan'=4,'freq'=2,'win'=2] {'chan'}, dimensions={0}, use_global_device_ids=true | all-gather | bytes 40960 | tf_op jit(solution)/shard_map/all_gather | solution.py:154
  56.6 1.5 pad_maximum_fusion
  58.1 2.0 %gather_fusion = bf16[4,1024,256]{2,1,0:T(8,128)(2,1)} fusion(bf16[4,1024,256]{2,1,0:T(8,128)(2,1)S(1)} %pad_maximum_fusion, s32[1024]{0:T(1024)S(1)} %pad_clamp_fusion), kind=kCustom, calls=%fused_computation | custom fusion | bytes 4194320 | tf_op jit(solution)/shard_map/jit(_take)/gather | solution.py:159
  60.1 4.1 %broadcast_select_fusion = bf16[2,2,1024,256]{3,1,2,0:T(2,128)(2,1)S(1)} fusion(pred[2,2]{1,0:T(4,128)(4,1)S(1)} %compare_and_fusion, bf16[2,2,1024,256]{3,2,1,0:T(8,128)(2,1)} %bitcast.56), kind=kLoop, calls=%fused_computation.2 | loop fusion | flops 1048576 | bytes 4194308 | tf_op jit(solution)/shard_map/jit(_take)/select_n | solution.py:159
  64.2 1.9 %copy.22 = bf16[256,8,2,256]{3,1,2,0:T(8,128)(2,1)} copy(bf16[256,8,2,256]{3,2,1,0:T(2,128)(2,1)S(1)} %bitcast.57) | data formatting | bytes 4194304
  66.1 11.1 %shard_map.65 = bf16[4,1024,256]{2,1,0:T(8,128)(2,1)} custom-call(s32[4096,2]{1,0:T(8,128)} %all_gather.3.pair_ref, bf16[2048,512]{1,0:T(8,128)(2,1)} %bitcast.55, f32[2,128]{1,0:T(2,128)} %fusion.6.rot_ref), custom_call_target="tpu_custom_call" | custom-call | tf_op jit(solution)/shard_map/pallas_call | solution.py:164
  77.2 2.2 %dynamic-slice_bitcast_fusion.1 = (bf16[1024,256]{1,0:T(8,128)(2,1)S(1)}, bf16[1024,256]{1,0:T(8,128)(2,1)}) fusion(bf16[4,1024,256]{2,1,0:T(8,128)(2,1)} %shard_map.65, s32[]{:T(128)S(6)} %min.25, s32[]{:T(128)S(6)} %min.28), kind=kLoop, calls=%fused_computation.18 | loop fusion | bytes 2097160 | tf_op jit(solution)/shard_map/jit(dynamic_index_in_dim)/squeeze | solution.py:178
  79.4 1.3 collective-permute-start.3
  80.7 1.5 collective-permute-start.6
  82.2 11.8 %collective-permute-done.3 = bf16[1024,256]{1,0:T(8,128)(2,1)S(1)} collective-permute-done((bf16[1024,256]{1,0:T(8,128)(2,1)S(1)}, bf16[1024,256]{1,0:T(8,128)(2,1)S(1)}, u32[]{:S(2)}, u32[]{:S(2)}) %collective-permute-start.3) | collective-permute-done | bytes 524320 | tf_op jit(solution)/shard_map/ppermute | solution.py:191
  94.2 1.9 %collective-permute-start.4 = (bf16[1024,256]{1,0:T(8,128)(2,1)S(1)}, bf16[1024,256]{1,0:T(8,128)(2,1)S(1)}, u32[]{:S(2)}, u32[]{:S(2)}) collective-permute-start(bf16[1024,256]{1,0:T(8,128)(2,1)S(1)} %fusion.2), channel_id=1, source_target_pairs={{0,4},{4,8},{1,5},{5,9},{2,6},{6,10},{3,7},{7,11},{16,20},{20,24},... | collective-permute-start | bytes 1572872 | tf_op jit(solution)/shard_map/ppermute | solution.py:191
  96.1 11.8 %collective-permute-done.4 = bf16[1024,256]{1,0:T(8,128)(2,1)S(1)} collective-permute-done((bf16[1024,256]{1,0:T(8,128)(2,1)S(1)}, bf16[1024,256]{1,0:T(8,128)(2,1)S(1)}, u32[]{:S(2)}, u32[]{:S(2)}) %collective-permute-start.4) | collective-permute-done | bytes 524320 | tf_op jit(solution)/shard_map/ppermute | solution.py:191
  107.9 2.3 %fusion.3 = (bf16[1024,256]{1,0:T(8,128)(2,1)}, bf16[1024,256]{1,0:T(8,128)(2,1)}) fusion(bf16[1024,256]{1,0:T(8,128)(2,1)S(1)} %collective-permute-done.4, bf16[4,1024,256]{2,1,0:T(8,128)(2,1)S(1)} %copy-done, s32[]{:T(128)S(6)} %min.23, bf16[1024,256]{1,0:T(8,128)(2,1)} %collective-permute-done.6, s32[]{:T(128)S(6)} %min.27), kind=kLoop, calls=%fused_computation.11 | loop fusion | flops 2097152 | bytes 3145736 | tf_op jit(solution)/shard_map/convert_element_type | solution.py:185
  111.5 4.0 %collective-permute-start.5 = (bf16[1024,256]{1,0:T(8,128)(2,1)}, bf16[1024,256]{1,0:T(8,128)(2,1)S(1)}, u32[]{:S(2)}, u32[]{:S(2)}) collective-permute-start(bf16[1024,256]{1,0:T(8,128)(2,1)} %get-tuple-element.5), channel_id=1, source_target_pairs={{0,4},{4,8},{8,12},{1,5},{5,9},{9,13},{2,6},{6,10},{10,14},{3,7},{... | collective-permute-start | bytes 1572872 | tf_op jit(solution)/shard_map/ppermute | solution.py:191
  115.5 7.8 %collective-permute-done.7 = bf16[1024,256]{1,0:T(8,128)(2,1)S(1)} collective-permute-done((bf16[1024,256]{1,0:T(8,128)(2,1)}, bf16[1024,256]{1,0:T(8,128)(2,1)S(1)}, u32[]{:S(2)}, u32[]{:S(2)}) %collective-permute-start.7) | collective-permute-done | bytes 524320 | tf_op jit(solution)/shard_map/ppermute | solution.py:192
  124.2 1.9 %collective-permute-start.8 = (bf16[1024,256]{1,0:T(8,128)(2,1)}, bf16[1024,256]{1,0:T(8,128)(2,1)S(1)}, u32[]{:S(2)}, u32[]{:S(2)}) collective-permute-start(bf16[1024,256]{1,0:T(8,128)(2,1)} %fusion.1), channel_id=1, source_target_pairs={{12,8},{8,4},{4,0},{13,9},{9,5},{5,1},{14,10},{10,6},{6,2},{15,11}... | collective-permute-start | bytes 1572872 | tf_op jit(solution)/shard_map/ppermute | solution.py:192
  126.1 10.3 %collective-permute-done.8 = bf16[1024,256]{1,0:T(8,128)(2,1)S(1)} collective-permute-done((bf16[1024,256]{1,0:T(8,128)(2,1)}, bf16[1024,256]{1,0:T(8,128)(2,1)S(1)}, u32[]{:S(2)}, u32[]{:S(2)}) %collective-permute-start.8) | collective-permute-done | bytes 524320 | tf_op jit(solution)/shard_map/ppermute | solution.py:192
  136.7 4.3 %collective-permute-start.9 = (bf16[256,256]{1,0:T(8,128)(2,1)S(1)}, bf16[256,256]{1,0:T(8,128)(2,1)S(1)}, u32[]{:S(2)}, u32[]{:S(2)}) collective-permute-start(bf16[256,256]{1,0:T(8,128)(2,1)S(1)} %get-tuple-element.16), channel_id=1, source_target_pairs={{0,1},{1,0},{2,3},{3,2},{4,5},{5,4},{6,7},{7,6},{8,9},{9,8},{10,11... | collective-permute-start | bytes 393224 | tf_op jit(solution)/shard_map/ppermute | solution.py:123
  142.7 3.3 %collective-permute-done.10 = bf16[256,256]{1,0:T(8,128)(2,1)S(1)} collective-permute-done((bf16[256,256]{1,0:T(8,128)(2,1)S(1)}, bf16[256,256]{1,0:T(8,128)(2,1)S(1)}, u32[]{:S(2)}, u32[]{:S(2)}) %collective-permute-start.10) | collective-permute-done | bytes 131104 | tf_op jit(solution)/shard_map/ppermute | solution.py:123
  145.9 3.1 %collective-permute-done.11 = bf16[256,256]{1,0:T(8,128)(2,1)S(1)} collective-permute-done((bf16[256,256]{1,0:T(8,128)(2,1)S(1)}, bf16[256,256]{1,0:T(8,128)(2,1)S(1)}, u32[]{:S(2)}, u32[]{:S(2)}) %collective-permute-start.11) | collective-permute-done | bytes 131104 | tf_op jit(solution)/shard_map/ppermute | solution.py:123
  150.7 1.7 %fusion.8 = f32[256,1000]{0,1:T(8,128)} fusion(bf16[256,1024]{0,1:T(8,128)(2,1)S(1)} %bitcast.59, bf16[1000,1024]{1,0:T(8,128)(2,1)S(1)} %copy-done.1), kind=kOutput, calls=%fused_computation.36 | convolution fusion | flops 524288000 | bytes 3596288 | tf_op jit(solution)/shard_map/dot_general | solution.py:201
  (35 shorter events, 10.5 us)
Async XLA Ops:
  11.4 4.8 %copy-start.3 = (s32[1024,2]{0,1:T(2,128)S(1)}, s32[1024,2]{0,1:T(2,128)}, u32[]{:S(2)}) copy-start(s32[1024,2]{0,1:T(2,128)} %param.7) | copy-start | bytes 24580
  13.9 41.9 %collective-permute-start = (bf16[1024,256]{1,0:T(8,128)(2,1)}, bf16[1024,256]{1,0:T(8,128)(2,1)S(1)}, u32[]{:S(2)}, u32[]{:S(2)}) collective-permute-start(bf16[1024,256]{1,0:T(8,128)(2,1)} %get-tuple-element.12), channel_id=1, source_target_pairs={{0,1},{1,0},{2,3},{3,2},{4,5},{5,4},{6,7},{7,6},{8,9},{9,8},{10,11... | collective-permute-start | bytes 1572872 | tf_op jit(solution)/shard_map/ppermute | solution.py:123
  14.6 41.3 %collective-permute-start.1 = (bf16[1024,256]{1,0:T(8,128)(2,1)S(1)}, bf16[1024,256]{1,0:T(8,128)(2,1)S(1)}, u32[]{:S(2)}, u32[]{:S(2)}) collective-permute-start(bf16[1024,256]{1,0:T(8,128)(2,1)S(1)} %get-tuple-element.11), channel_id=1, source_target_pairs={{0,2},{1,3},{2,0},{3,1},{4,6},{5,7},{6,4},{7,5},{8,10},{9,11},{10,... | collective-permute-start | bytes 1572872 | tf_op jit(solution)/shard_map/ppermute | solution.py:123
  15.8 40.1 %collective-permute-start.2 = (bf16[1024,256]{1,0:T(8,128)(2,1)S(1)}, bf16[1024,256]{1,0:T(8,128)(2,1)}, u32[]{:S(2)}, u32[]{:S(2)}) collective-permute-start(bf16[1024,256]{1,0:T(8,128)(2,1)S(1)} %get-tuple-element.10), channel_id=1, source_target_pairs={{0,3},{1,2},{2,1},{3,0},{4,7},{5,6},{6,5},{7,4},{8,11},{9,10},{10,... | collective-permute-start | bytes 1572872 | tf_op jit(solution)/shard_map/ppermute | solution.py:123
  55.8 0.8 copy-start.2
  77.2 16.8 %copy-start = (bf16[4,1024,256]{2,1,0:T(8,128)(2,1)S(1)}, bf16[4,1024,256]{2,1,0:T(8,128)(2,1)}, u32[]{:S(2)}) copy-start(bf16[4,1024,256]{2,1,0:T(8,128)(2,1)} %shard_map.65) | copy-start | bytes 6291460
  79.4 14.6 %collective-permute-start.3 = (bf16[1024,256]{1,0:T(8,128)(2,1)S(1)}, bf16[1024,256]{1,0:T(8,128)(2,1)S(1)}, u32[]{:S(2)}, u32[]{:S(2)}) collective-permute-start(bf16[1024,256]{1,0:T(8,128)(2,1)S(1)} %get-tuple-element.7), channel_id=1, source_target_pairs={{0,4},{1,5},{2,6},{3,7},{16,20},{17,21},{18,22},{19,23}} | collective-permute-start | bytes 1572872 | tf_op jit(solution)/shard_map/ppermute | solution.py:191
  80.7 15.4 %collective-permute-start.6 = (bf16[1024,256]{1,0:T(8,128)(2,1)}, bf16[1024,256]{1,0:T(8,128)(2,1)}, u32[]{:S(2)}, u32[]{:S(2)}) collective-permute-start(bf16[1024,256]{1,0:T(8,128)(2,1)} %get-tuple-element.8), channel_id=1, source_target_pairs={{12,8},{13,9},{14,10},{15,11},{28,24},{29,25},{30,26},{31,27}} | collective-permute-start | bytes 1572872 | tf_op jit(solution)/shard_map/ppermute | solution.py:192
  94.2 13.8 %collective-permute-start.4 = (bf16[1024,256]{1,0:T(8,128)(2,1)S(1)}, bf16[1024,256]{1,0:T(8,128)(2,1)S(1)}, u32[]{:S(2)}, u32[]{:S(2)}) collective-permute-start(bf16[1024,256]{1,0:T(8,128)(2,1)S(1)} %fusion.2), channel_id=1, source_target_pairs={{0,4},{4,8},{1,5},{5,9},{2,6},{6,10},{3,7},{7,11},{16,20},{20,24},... | collective-permute-start | bytes 1572872 | tf_op jit(solution)/shard_map/ppermute | solution.py:191
  110.2 13.1 %collective-permute-start.7 = (bf16[1024,256]{1,0:T(8,128)(2,1)}, bf16[1024,256]{1,0:T(8,128)(2,1)S(1)}, u32[]{:S(2)}, u32[]{:S(2)}) collective-permute-start(bf16[1024,256]{1,0:T(8,128)(2,1)} %get-tuple-element.6), channel_id=1, source_target_pairs={{12,8},{8,4},{13,9},{9,5},{14,10},{10,6},{15,11},{11,7},{28,24},{2... | collective-permute-start | bytes 1572872 | tf_op jit(solution)/shard_map/ppermute | solution.py:192
  111.5 14.7 %collective-permute-start.5 = (bf16[1024,256]{1,0:T(8,128)(2,1)}, bf16[1024,256]{1,0:T(8,128)(2,1)S(1)}, u32[]{:S(2)}, u32[]{:S(2)}) collective-permute-start(bf16[1024,256]{1,0:T(8,128)(2,1)} %get-tuple-element.5), channel_id=1, source_target_pairs={{0,4},{4,8},{8,12},{1,5},{5,9},{9,13},{2,6},{6,10},{10,14},{3,7},{... | collective-permute-start | bytes 1572872 | tf_op jit(solution)/shard_map/ppermute | solution.py:191
  124.2 12.2 %collective-permute-start.8 = (bf16[1024,256]{1,0:T(8,128)(2,1)}, bf16[1024,256]{1,0:T(8,128)(2,1)S(1)}, u32[]{:S(2)}, u32[]{:S(2)}) collective-permute-start(bf16[1024,256]{1,0:T(8,128)(2,1)} %fusion.1), channel_id=1, source_target_pairs={{12,8},{8,4},{4,0},{13,9},{9,5},{5,1},{14,10},{10,6},{6,2},{15,11}... | collective-permute-start | bytes 1572872 | tf_op jit(solution)/shard_map/ppermute | solution.py:192
  136.7 6.0 %collective-permute-start.9 = (bf16[256,256]{1,0:T(8,128)(2,1)S(1)}, bf16[256,256]{1,0:T(8,128)(2,1)S(1)}, u32[]{:S(2)}, u32[]{:S(2)}) collective-permute-start(bf16[256,256]{1,0:T(8,128)(2,1)S(1)} %get-tuple-element.16), channel_id=1, source_target_pairs={{0,1},{1,0},{2,3},{3,2},{4,5},{5,4},{6,7},{7,6},{8,9},{9,8},{10,11... | collective-permute-start | bytes 393224 | tf_op jit(solution)/shard_map/ppermute | solution.py:123
  141.0 5.0 %collective-permute-start.10 = (bf16[256,256]{1,0:T(8,128)(2,1)S(1)}, bf16[256,256]{1,0:T(8,128)(2,1)S(1)}, u32[]{:S(2)}, u32[]{:S(2)}) collective-permute-start(bf16[256,256]{1,0:T(8,128)(2,1)S(1)} %get-tuple-element.15), channel_id=1, source_target_pairs={{0,2},{1,3},{2,0},{3,1},{4,6},{5,7},{6,4},{7,5},{8,10},{9,11},{10,... | collective-permute-start | bytes 393224 | tf_op jit(solution)/shard_map/ppermute | solution.py:123
  142.2 6.8 %collective-permute-start.11 = (bf16[256,256]{1,0:T(8,128)(2,1)S(1)}, bf16[256,256]{1,0:T(8,128)(2,1)S(1)}, u32[]{:S(2)}, u32[]{:S(2)}) collective-permute-start(bf16[256,256]{1,0:T(8,128)(2,1)S(1)} %get-tuple-element.14), channel_id=1, source_target_pairs={{0,3},{1,2},{2,1},{3,0},{4,7},{5,6},{6,5},{7,4},{8,11},{9,10},{10,... | collective-permute-start | bytes 393224 | tf_op jit(solution)/shard_map/ppermute | solution.py:123
  149.1 1.6 %copy-start.1 = (bf16[1000,1024]{1,0:T(8,128)(2,1)S(1)}, bf16[1000,1024]{1,0:T(8,128)(2,1)}, u32[]{:S(2)}) copy-start(bf16[1000,1024]{1,0:T(8,128)(2,1)} %constant.110.table_ref) | copy-start | bytes 6144004
